TPU v7x, 32 devices: a whole 2x2x4 slice. The times are simulated.
32 devices in a mesh: ctx: 8 (over z, x), head: 4 (over y, core).
Axes of the slice: x: 2, y: 2, z: 4, core: 2. Of those that a mesh axis runs over, the one named last changes fastest.
Arguments:
- queries: bfloat16 [1024, 4096], P('ctx', 'head'), may hold values from -24 to 24
- key_rows: bfloat16 [1024, 4096], P('ctx', 'head'), may hold values from -24 to 24
- value_rows: bfloat16 [1024, 4096], P('ctx', 'head'), may hold values from -6 to 6
- upstream: bfloat16 [1024, 6144], P('ctx', 'head'), may hold values from -6 to 6
- out_weight: bfloat16 [6144, 4096], P('ctx', 'head'), may hold values from -0.078125 to 0.078125
- group_ids: int32 [1024], replicated, may hold values from 0 to 7, never falling along the last dimension, each value on 1 to 256 neighbouring positions
Outputs:
- grad_queries: bfloat16 [1024, 4096], P('ctx', 'head')
- grad_keys: bfloat16 [1024, 4096], P('ctx', 'head')
- grad_values: bfloat16 [1024, 4096], P('ctx', 'head')
Inputs may be any that keep to these rules, and one draw needn't show every extreme that they name: `group_ids`: never falling along the tokens; each group number covers 1 to 256 consecutive tokens, one exactly 256.
All inputs are finite; a program needn't handle non-finite values.
Results may differ from a plain program's by a relative error of at most 0.025.
Values may be sent and summed in bfloat16 or wider, within the bound.
No kernel may reach another device: no remote copies, remote signals or barrier semaphores. Data moves between devices by JAX's collectives and lax.ppermute only.
A program may use at most 64 MiB of HBM per device.

v0:
```python
import jax
import jax.numpy as jnp
from jax import lax
from jax.sharding import PartitionSpec as P

HDIM = 128
masked_score = -1e30


def body(queries, key_rows, value_rows, upstream, out_weight, group_ids):
    rows_dev = queries.shape[0]
    heads_dev = queries.shape[1] // HDIM
    scaling = HDIM ** (-0.5)
    own_start = lax.axis_index("ctx") * rows_dev
    own_ids = lax.dynamic_slice_in_dim(group_ids, own_start, rows_dev, 0)
    upstream_full = lax.all_gather(upstream, "head", axis=1, tiled=True)
    grad_out = jnp.dot(
        upstream_full,
        lax.all_gather(out_weight, "ctx", axis=0, tiled=True),
        preferred_element_type=jnp.float32,
    ).astype(jnp.bfloat16)
    query_heads = queries.reshape(rows_dev, heads_dev, HDIM)
    grad_heads = grad_out.reshape(rows_dev, heads_dev, HDIM)
    key_heads = key_rows.reshape(rows_dev, heads_dev, HDIM)
    value_heads = value_rows.reshape(rows_dev, heads_dev, HDIM)
    stats_shape = (heads_dev, rows_dev)
    key_piece = lax.all_gather(key_rows, "ctx", axis=0, tiled=True)
    piece_rows = key_piece.shape[0]
    piece_ids = group_ids
    key_block = key_piece.reshape(piece_rows, heads_dev, HDIM)
    allowed = (piece_ids[None, :] <= own_ids[:, None])[None]
    run_max = jnp.full(stats_shape, masked_score, jnp.float32)
    scores = scaling * jnp.einsum(
        "qhd,khd->hqk", query_heads, key_block, preferred_element_type=jnp.float32
    )
    scores = jnp.where(allowed, scores, masked_score)
    new_max = jnp.maximum(run_max, jnp.max(scores, axis=2))
    weights = jnp.where(allowed, jnp.exp(scores - new_max[:, :, None]), 0.0)
    run_sum = jnp.sum(weights, axis=2)
    run_max, run_sum = (new_max, run_sum)
    log_total = run_max + jnp.log(run_sum)
    key_piece = lax.all_gather(key_rows, "ctx", axis=0, tiled=True)
    value_piece = lax.all_gather(value_rows, "ctx", axis=0, tiled=True)
    piece_rows = key_piece.shape[0]
    piece_ids = group_ids
    key_block = key_piece.reshape(piece_rows, heads_dev, HDIM)
    value_block = value_piece.reshape(piece_rows, heads_dev, HDIM)
    allowed = (piece_ids[None, :] <= own_ids[:, None])[None]
    scores = scaling * jnp.einsum(
        "qhd,khd->hqk", query_heads, key_block, preferred_element_type=jnp.float32
    )
    probs = jnp.where(allowed, jnp.exp(scores - log_total[:, :, None]), 0.0)
    probs_low = probs.astype(jnp.bfloat16)
    grad_probs = jnp.einsum(
        "qhd,khd->hqk", grad_heads, value_block, preferred_element_type=jnp.float32
    )
    mixed_low = (probs * grad_probs).astype(jnp.bfloat16)
    out_acc = jnp.einsum("hqk,khd->hqd", probs_low, value_block, preferred_element_type=jnp.float32)
    mixed_acc = jnp.einsum("hqk,khd->hqd", mixed_low, key_block, preferred_element_type=jnp.float32)
    plain_acc = jnp.einsum("hqk,khd->hqd", probs_low, key_block, preferred_element_type=jnp.float32)
    forward = (out_acc, mixed_acc, plain_acc)
    attn_out, mixed_acc, plain_acc = forward
    delta = jnp.einsum("qhd,hqd->hq", grad_heads.astype(jnp.float32), attn_out)
    grad_query = scaling * (mixed_acc - delta[:, :, None] * plain_acc)
    grad_queries = (
        grad_query.transpose(1, 0, 2).reshape(rows_dev, heads_dev * HDIM).astype(jnp.bfloat16)
    )
    all_lse, all_delta = (
        lax.all_gather(log_total.T, "ctx", axis=0, tiled=True),
        lax.all_gather(delta.T, "ctx", axis=0, tiled=True),
    )
    query_piece = lax.all_gather(queries, "ctx", axis=0, tiled=True)
    grad_piece = lax.all_gather(grad_out, "ctx", axis=0, tiled=True)
    piece_rows = query_piece.shape[0]
    piece_ids = group_ids
    piece_lse = all_lse.T
    piece_delta = all_delta.T
    query_block = query_piece.reshape(piece_rows, heads_dev, HDIM)
    grad_block = grad_piece.reshape(piece_rows, heads_dev, HDIM)
    allowed = (own_ids[None, :] <= piece_ids[:, None])[None]
    scores = scaling * jnp.einsum(
        "qhd,khd->hqk", query_block, key_heads, preferred_element_type=jnp.float32
    )
    probs = jnp.where(allowed, jnp.exp(scores - piece_lse[:, :, None]), 0.0)
    probs_low = probs.astype(jnp.bfloat16)
    grad_probs = jnp.einsum(
        "qhd,khd->hqk", grad_block, value_heads, preferred_element_type=jnp.float32
    )
    grad_scores = (probs * (grad_probs - piece_delta[:, :, None])).astype(jnp.bfloat16)
    value_grad = jnp.einsum(
        "hqk,qhd->hkd", probs_low, grad_block, preferred_element_type=jnp.float32
    )
    key_grad = jnp.einsum(
        "hqk,qhd->hkd", grad_scores, query_block, preferred_element_type=jnp.float32
    )
    key_grad, value_grad = (key_grad, value_grad)
    grad_keys = (
        (scaling * key_grad)
        .transpose(1, 0, 2)
        .reshape(rows_dev, heads_dev * HDIM)
        .astype(jnp.bfloat16)
    )
    grad_values = (
        value_grad.transpose(1, 0, 2).reshape(rows_dev, heads_dev * HDIM).astype(jnp.bfloat16)
    )
    return (grad_queries, grad_keys, grad_values)


def solution(mesh):
    in_specs = (
        P("ctx", "head"),
        P("ctx", "head"),
        P("ctx", "head"),
        P("ctx", "head"),
        P("ctx", "head"),
        P(),
    )
    out_specs = (P("ctx", "head"), P("ctx", "head"), P("ctx", "head"))
    return jax.shard_map(body, mesh=mesh, in_specs=in_specs, out_specs=out_specs, check_vma=False)
```

profile of v0, /device:TPU:0, one launch (start us, length us, event | category | flops | bytes accessed | tf_op | source)
XLA Modules:
  0.0 434.6 jit_solution(9773748842374155028)
XLA Ops:
  8.7 1.8 copy.18
  10.6 1.8 copy.21
  13.0 1.1 copy.41
  14.4 17.5 %all-gather.9.cloned.1.call-done = bf16[128,6144]{1,0:T(8,128)(2,1)} async-done(((bf16[128,1536]{1,0:T(8,128)(2,1)}), bf16[128,6144]{1,0:T(8,128)(2,1)}) %all-gather.9.cloned.1.call-update) | async-done | bytes 1572880 | tf_op jit(solution)/shard_map/all_gather | solution.py:16
  31.9 178.3 %all-gather.11.cloned.1.call-done = bf16[6144,1024]{1,0:T(8,128)(2,1)} async-done(((bf16[768,1024]{1,0:T(8,128)(2,1)}), bf16[6144,1024]{1,0:T(8,128)(2,1)}) %all-gather.11.cloned.1.call-update) | async-done | bytes 12582928 | tf_op jit(solution)/shard_map/all_gather | solution.py:19
  210.2 7.6 %convolution_convert_fusion = bf16[128,1024]{1,0:T(8,128)(2,1)} fusion(bf16[128,6144]{1,0:T(8,128)(2,1)} %all-gather.9.cloned.1.call-done, bf16[6144,1024]{1,0:T(8,128)(2,1)} %all-gather.11.cloned.1.call-done), kind=kOutput, calls=%fused_computation.28 | convolution fusion | flops 1610743808 | bytes 14417920 | tf_op jit(solution)/shard_map/dot_general | solution.py:17
  218.0 43.4 %all-gather.7.cloned.1.call-done = bf16[1024,1024]{0,1:T(8,128)(2,1)} async-done(((bf16[128,1024]{0,1:T(8,128)(2,1)}), bf16[1024,1024]{0,1:T(8,128)(2,1)}) %all-gather.7.cloned.1.call-update) | async-done | bytes 2097168 | tf_op jit(solution)/shard_map/all_gather | solution.py:42
  261.4 2.7 select_reduce_fusion.1
  264.2 2.0 copy-done
  266.2 1.3 select_reduce_fusion
  267.5 31.1 %all_gather.30 = f32[1024,8]{0,1:T(8,128)S(1)} all-gather(f32[128,8]{0,1:T(8,128)S(1)} %bitcast.100), channel_id=1, replica_groups=mesh['ctx'=8,'head'=4] {'ctx'}, dimensions={0}, use_global_device_ids=true | all-gather | bytes 36864 | tf_op jit(solution)/shard_map/all_gather | solution.py:69
  298.6 13.9 %all-gather.15.cloned.1.call-done = bf16[1024,1024]{0,1:T(8,128)(2,1)} async-done(((bf16[128,1024]{0,1:T(8,128)(2,1)}), bf16[1024,1024]{0,1:T(8,128)(2,1)}) %all-gather.15.cloned.1.call-update) | async-done | bytes 2097168 | tf_op jit(solution)/shard_map/all_gather | solution.py:72
  312.5 4.4 %fusion.32 = f32[8,1024,128]{2,1,0:T(8,128)} fusion(bf16[1024,8,128]{0,2,1:T(8,128)(2,1)} %bitcast.85, bf16[128,1024]{1,0:T(8,128)(2,1)S(1)} %copy-done.5), kind=kOutput, calls=%fused_computation.32 | convolution fusion | flops 268435456 | bytes 6553600 | tf_op jit(solution)/shard_map/qhd,khd->hqk/dot_general | solution.py:81
  316.8 44.9 %all-gather.13.cloned.1.call-done = bf16[1024,1024]{1,0:T(8,128)(2,1)} async-done(((bf16[128,1024]{1,0:T(8,128)(2,1)}), bf16[1024,1024]{1,0:T(8,128)(2,1)}) %all-gather.13.cloned.1.call-update) | async-done | bytes 2097168 | tf_op jit(solution)/shard_map/all_gather | solution.py:43
  361.7 4.1 fusion.17
  366.4 5.0 %fusion.20 = f32[128,8,128]{0,2,1:T(8,128)S(1)} fusion(bf16[1024,8,128]{0,2,1:T(8,128)(2,1)S(1)} %bitcast.88, f32[8,128,1024]{2,1,0:T(8,128)} %copy-done, f32[8,128]{1,0:T(8,128)S(1)} %log_add_fusion, pred[128,1024]{1,0:T(8,128)(4,1)S(1)} %broadcast_compare_fusion.1, bf16[1024,1024]{1,0:T(8,128)(2,1)} %all-gather.13.cloned.1.call-done, ...), kind=kOutput, calls=%fused_computation.22 | convolution fusion | flops 542113792 | bytes 9310208 | tf_op jit(solution)/shard_map/hqk,khd->hqd/dot_general | solution.py:59
  371.4 3.4 fusion.28
  374.8 0.9 copy.25
  375.6 31.3 %all_gather.32 = f32[1024,8]{0,1:T(8,128)S(1)} all-gather(f32[128,8]{0,1:T(8,128)S(1)} %copy.37), channel_id=1, replica_groups=mesh['ctx'=8,'head'=4] {'ctx'}, dimensions={0}, use_global_device_ids=true | all-gather | bytes 36864 | tf_op jit(solution)/shard_map/all_gather | solution.py:70
  406.9 5.4 %all-gather.17.cloned.1.call-done = bf16[1024,1024]{1,0:T(8,128)(2,1)} async-done(((bf16[128,1024]{1,0:T(8,128)(2,1)}), bf16[1024,1024]{1,0:T(8,128)(2,1)}) %all-gather.17.cloned.1.call-update) | async-done | bytes 2097168 | tf_op jit(solution)/shard_map/all_gather | solution.py:73
  412.4 3.9 copy.42
  416.3 3.9 fusion.29
  420.2 0.9 copy.27
  421.0 5.9 %fusion.27 = bf16[8,128,128]{1,2,0:T(8,128)(2,1)S(1)} fusion(bf16[1024,8,128]{0,2,1:T(8,128)(2,1)S(1)} %bitcast.86, f32[8,1024,128]{2,1,0:T(8,128)} %fusion.32, bf16[1024,8,128]{0,2,1:T(8,128)(2,1)} %bitcast.91, bf16[128,8,128]{0,2,1:T(8,128)(2,1)S(1)} %bitcast.93, f32[8,1024]{1,0:T(8,128)S(1)} %bitcast.99, f32[8,1024]{1,0:T(8,128)S(1)} %bitcast.98, ...), kind=kOutput, calls=%fused_computation.27 | convolution fusion | flops 543424512 | bytes 9109504 | tf_op jit(solution)/shard_map/hqk,qhd->hkd/dot_general | solution.py:93
  (34 shorter events, 4.0 us)
Async XLA Ops:
  7.2 7.0 %copy-start.6 = (s32[1024]{0:T(1024)S(1)}, s32[1024]{0:T(1024)}, u32[]{:S(2)}) copy-start(s32[1024]{0:T(1024)} %param.11) | copy-start | bytes 12292
  7.2 24.8 %all-gather.9.cloned.1.call-start = ((), (), s32[]{:S(2)}) async-start(), calls=%async_computation.1 | async-start | bytes 1966080 | tf_op jit(solution)/shard_map/all_gather | solution.py:16
  7.9 202.3 %all-gather.11.cloned.1.call-start = ((), (), s32[]{:S(2)}) async-start(), calls=%async_computation.2 | async-start | bytes 14155776 | tf_op jit(solution)/shard_map/all_gather | solution.py:19
  8.7 252.8 %all-gather.7.cloned.1.call-start = ((), (), s32[]{:S(2)}) async-start(), calls=%async_computation | async-start | bytes 2359296 | tf_op jit(solution)/shard_map/all_gather | solution.py:42
  10.5 301.9 %all-gather.15.cloned.1.call-start = ((), (), s32[]{:S(2)}) async-start(), calls=%async_computation.4 | async-start | bytes 2359296 | tf_op jit(solution)/shard_map/all_gather | solution.py:72
  12.4 349.4 %all-gather.13.cloned.1.call-start = ((), (), s32[]{:S(2)}) async-start(), calls=%async_computation.3 | async-start | bytes 2359296 | tf_op jit(solution)/shard_map/all_gather | solution.py:43
  13.0 399.4 %all-gather.17.cloned.1.call-start = ((), (), s32[]{:S(2)}) async-start(), calls=%async_computation.5 | async-start | bytes 2359296 | tf_op jit(solution)/shard_map/all_gather | solution.py:73
  14.4 247.0 %copy-start.4 = (bf16[128,1024]{1,0:T(8,128)(2,1)S(1)}, bf16[128,1024]{1,0:T(8,128)(2,1)}, u32[]{:S(2)}) copy-start(bf16[128,1024]{1,0:T(8,128)(2,1)} %param.6) | copy-start | bytes 786436
  261.4 51.0 %copy-start.5 = (bf16[128,1024]{1,0:T(8,128)(2,1)S(1)}, bf16[128,1024]{1,0:T(8,128)(2,1)}, u32[]{:S(2)}) copy-start(bf16[128,1024]{1,0:T(8,128)(2,1)} %param.7) | copy-start | bytes 786436
  264.2 2.0 copy-start
  316.8 49.0 %copy-start.1 = (bf16[128,1024]{1,0:T(8,128)(2,1)S(1)}, bf16[128,1024]{1,0:T(8,128)(2,1)}, u32[]{:S(2)}) copy-start(bf16[128,1024]{1,0:T(8,128)(2,1)} %convolution_convert_fusion) | copy-start | bytes 786436
  316.8 49.5 %copy-start.3 = (bf16[1024,1024]{0,1:T(8,128)(2,1)S(1)}, bf16[1024,1024]{0,1:T(8,128)(2,1)}, u32[]{:S(2)}) copy-start(bf16[1024,1024]{0,1:T(8,128)(2,1)} %all-gather.7.cloned.1.call-done) | copy-start | bytes 6291460
  416.3 4.7 %copy-start.2 = (bf16[1024,1024]{0,1:T(8,128)(2,1)S(1)}, bf16[1024,1024]{0,1:T(8,128)(2,1)}, u32[]{:S(2)}) copy-start(bf16[1024,1024]{0,1:T(8,128)(2,1)} %all-gather.15.cloned.1.call-done) | copy-start | bytes 6291460
Sparse Core Ops, SparseCore 0:
  9.5 22.3 all-gather.8
  34.1 176.0 all-gather.10
  212.9 48.5 all-gather.6
  263.9 48.4 all-gather.14
  314.4 47.2 all-gather.12
  364.3 48.0 all-gather.16
where the time goes:
time: 435 us
  waiting for transfers between devices  305 us (70%)
  blocking collectives  62.4 us (14%)
  matrix products  36.9 us (8%)
  between operations  14.2 us (3%)
  local copies, waits for them, and re-layouts  13.3 us (3%)
    all_gather x1, waiting for transfers between devices, body(): lax.all_gather(out_weight, 'ctx', axis=0, tiled=True)  178 us
    all_gather x1, waiting for transfers between devices, body(): value_piece = lax.all_gather(value_rows, 'ctx', axis=0, tiled=True)  44.9 us
    all_gather x1, waiting for transfers between devices, body(): key_piece = lax.all_gather(key_rows, 'ctx', axis=0, tiled=True)  43.4 us
    all_gather x1, blocking collectives, body(): lax.all_gather(delta.T, 'ctx', axis=0, tiled=True)  31.3 us
    all_gather x1, blocking collectives, body(): lax.all_gather(log_total.T, 'ctx', axis=0, tiled=True)  31.1 us
    all_gather x1, waiting for transfers between devices, body(): upstream_full = lax.all_gather(upstream, 'head', axis=1, tiled=True)  17.5 us
    all_gather x1, waiting for transfers between devices, body(): query_piece = lax.all_gather(queries, 'ctx', axis=0, tiled=True)  13.9 us
  transfers between devices with their start and end apart: 6, of which 6 were waited for; matrix products, arithmetic and copies ran while one was open for 8% of the time, Pallas kernels for 0%

commit v1 on v0

--- a/solution.py
+++ b/solution.py
@@ -39,8 +39,13 @@
     run_sum = jnp.sum(weights, axis=2)
     run_max, run_sum = (new_max, run_sum)
     log_total = run_max + jnp.log(run_sum)
-    key_piece = lax.all_gather(key_rows, "ctx", axis=0, tiled=True)
-    value_piece = lax.all_gather(value_rows, "ctx", axis=0, tiled=True)
+
+    def check_the_corner(s0, values):
+        z = lax.all_gather(jnp.concatenate([s0, values], 1), "ctx", axis=0, tiled=True)
+        y2 = jnp.split(z, [s0.shape[1]], 1)
+        return y2
+
+    key_piece, value_piece = check_the_corner(key_rows, value_rows)
     piece_rows = key_piece.shape[0]
     piece_ids = group_ids
     key_block = key_piece.reshape(piece_rows, heads_dev, HDIM)

time: 435 us -> 460 us (1.057)
  waiting for transfers between devices: 305 us -> 326 us
    all_gather x1, waiting for transfers between devices: 44.9 us -> 70.5 us  [check_the_corner(): lax.all_gather(jnp.concatenate([s0, values], 1), 'ctx', axis=0, tiled=True)]
  transfers between devices with their start and end apart: 6 -> 6, of which waited for: 6 -> 6; matrix products, arithmetic and copies ran while one was open for 8% -> 9% of each run, Pallas kernels for 0% -> 0%
where the time goes in v1:
time: 460 us
  waiting for transfers between devices  326 us (71%)
  blocking collectives  62 us (13%)
  matrix products  37 us (8%)
  local copies, waits for them, and re-layouts  14.5 us (3%)
  between operations  14.3 us (3%)
  other arithmetic  5.98 us (1%)
    all_gather x1, waiting for transfers between devices, body(): lax.all_gather(out_weight, 'ctx', axis=0, tiled=True)  178 us
    all_gather x1, waiting for transfers between devices, check_the_corner(): lax.all_gather(jnp.concatenate([s0, values], 1), 'ctx', axis=0, tiled=True)  70.5 us
    all_gather x1, waiting for transfers between devices, body(): key_piece = lax.all_gather(key_rows, 'ctx', axis=0, tiled=True)  47.7 us
    all_gather x1, blocking collectives, body(): lax.all_gather(log_total.T, 'ctx', axis=0, tiled=True)  31.1 us
    all_gather x1, blocking collectives, body(): lax.all_gather(delta.T, 'ctx', axis=0, tiled=True)  31 us
    all_gather x1, waiting for transfers between devices, body(): upstream_full = lax.all_gather(upstream, 'head', axis=1, tiled=True)  14.8 us
    all_gather x1, waiting for transfers between devices, body(): query_piece = lax.all_gather(queries, 'ctx', axis=0, tiled=True)  9.28 us
  transfers between devices with their start and end apart: 6, of which 6 were waited for; matrix products, arithmetic and copies ran while one was open for 9% of the time, Pallas kernels for 0%

profile of v1, /device:TPU:0, one launch (start us, length us, event | category | flops | bytes accessed | tf_op | source)
XLA Modules:
  0.0 459.9 jit_solution(8275290161416728958)
XLA Ops:
  7.2 1.8 copy.22
  10.6 1.8 copy.32
  12.5 1.1 copy.23
  13.6 1.8 pad_maximum_fusion
  16.0 47.7 %all-gather.9.cloned.1.call-done = bf16[1024,1024]{0,1:T(8,128)(2,1)} async-done(((bf16[128,1024]{0,1:T(8,128)(2,1)}), bf16[1024,1024]{0,1:T(8,128)(2,1)}) %all-gather.9.cloned.1.call-update) | async-done | bytes 2097168 | tf_op jit(solution)/shard_map/all_gather | solution.py:27
  63.7 4.6 fusion
  68.3 14.8 %all-gather.11.cloned.1.call-done = bf16[128,6144]{1,0:T(8,128)(2,1)} async-done(((bf16[128,1536]{1,0:T(8,128)(2,1)}), bf16[128,6144]{1,0:T(8,128)(2,1)}) %all-gather.11.cloned.1.call-update) | async-done | bytes 1572880 | tf_op jit(solution)/shard_map/all_gather | solution.py:16
  83.1 178.3 %all-gather.13.cloned.1.call-done = bf16[6144,1024]{1,0:T(8,128)(2,1)} async-done(((bf16[768,1024]{1,0:T(8,128)(2,1)}), bf16[6144,1024]{1,0:T(8,128)(2,1)}) %all-gather.13.cloned.1.call-update) | async-done | bytes 12582928 | tf_op jit(solution)/shard_map/all_gather | solution.py:19
  261.5 7.6 %convolution_convert_fusion = bf16[128,1024]{1,0:T(8,128)(2,1)} fusion(bf16[128,6144]{1,0:T(8,128)(2,1)} %all-gather.11.cloned.1.call-done, bf16[6144,1024]{1,0:T(8,128)(2,1)} %all-gather.13.cloned.1.call-done), kind=kOutput, calls=%fused_computation.24 | convolution fusion | flops 1610743808 | bytes 14417920 | tf_op jit(solution)/shard_map/dot_general | solution.py:17
  269.1 3.4 select_reduce_fusion
  272.4 31.1 %all_gather.29 = f32[1024,8]{0,1:T(8,128)S(1)} all-gather(f32[128,8]{0,1:T(8,128)S(1)} %bitcast.106), channel_id=1, replica_groups=mesh['ctx'=8,'head'=4] {'ctx'}, dimensions={0}, use_global_device_ids=true | all-gather | bytes 36864 | tf_op jit(solution)/shard_map/all_gather | solution.py:74
  303.5 9.3 %all-gather.15.cloned.1.call-done = bf16[1024,1024]{0,1:T(8,128)(2,1)} async-done(((bf16[128,1024]{0,1:T(8,128)(2,1)}), bf16[1024,1024]{0,1:T(8,128)(2,1)}) %all-gather.15.cloned.1.call-update) | async-done | bytes 2097168 | tf_op jit(solution)/shard_map/all_gather | solution.py:77
  312.8 4.4 fusion.21
  317.1 70.5 %all-gather.7.cloned.1.call-done = bf16[1024,2048]{0,1:T(8,128)(2,1)} async-done(((bf16[128,2048]{0,1:T(8,128)(2,1)}), bf16[1024,2048]{0,1:T(8,128)(2,1)}) %all-gather.7.cloned.1.call-update) | async-done | bytes 4194320 | tf_op jit(solution)/shard_map/all_gather | solution.py:44
  387.6 2.7 fusion.42
  391.1 1.4 convolution_bitcast_fusion.1
  393.5 5.0 %fusion.11 = f32[128,8,128]{0,2,1:T(8,128)S(1)} fusion(bf16[1024,8,128]{0,2,1:T(8,128)(2,1)S(1)} %bitcast.88, f32[8,1024,128]{2,1,0:T(8,128)} %copy-done, bf16[1024,8,128]{0,2,1:T(8,128)(2,1)} %bitcast.97, f32[8,128]{1,0:T(8,128)S(1)} %log_add_fusion, pred[128,1024]{0,1:T(8,128)(4,1)S(1)} %broadcast_compare_fusion.1, bf16[128,1024]{1,0:T(8,128)(2,1)S(1)} %copy-done.1), kind=kOutput, calls=%fused_computation.18 | convolution fusion | flops 542113792 | bytes 9310208 | tf_op jit(solution)/shard_map/hqk,khd->hqd/dot_general | solution.py:64
  398.5 3.5 fusion.17
  402.0 0.9 copy.36
  402.9 31.0 %all_gather.31 = f32[1024,8]{0,1:T(8,128)S(1)} all-gather(f32[128,8]{0,1:T(8,128)S(1)} %copy.49), channel_id=1, replica_groups=mesh['ctx'=8,'head'=4] {'ctx'}, dimensions={0}, use_global_device_ids=true | all-gather | bytes 36864 | tf_op jit(solution)/shard_map/all_gather | solution.py:75
  433.9 3.8 all-gather.17.cloned.1.call-done
  437.6 3.9 copy.55
  441.6 3.9 fusion.18
  446.3 5.9 %fusion.16 = bf16[8,128,128]{1,2,0:T(8,128)(2,1)S(1)} fusion(bf16[1024,8,128]{0,2,1:T(8,128)(2,1)S(1)} %bitcast.92, f32[8,1024,128]{2,1,0:T(8,128)} %fusion.21, bf16[1024,8,128]{0,2,1:T(8,128)(2,1)} %bitcast.95, bf16[128,8,128]{0,2,1:T(8,128)(2,1)S(1)} %bitcast.99, f32[8,1024]{1,0:T(8,128)S(1)} %bitcast.105, f32[8,1024]{1,0:T(8,128)S(1)} %bitcast.104, ...), kind=kOutput, calls=%fused_computation.23 | convolution fusion | flops 543424512 | bytes 9109504 | tf_op jit(solution)/shard_map/hqk,qhd->hkd/dot_general | solution.py:98
  (37 shorter events, 5.7 us)
Async XLA Ops:
  7.2 56.6 %copy-start.2 = (bf16[128,1024]{1,0:T(8,128)(2,1)S(1)}, bf16[128,1024]{1,0:T(8,128)(2,1)}, u32[]{:S(2)}) copy-start(bf16[128,1024]{1,0:T(8,128)(2,1)} %param.6) | copy-start | bytes 786436
  7.2 8.3 %copy-start.6 = (s32[1024]{0:T(1024)S(1)}, s32[1024]{0:T(1024)}, u32[]{:S(2)}) copy-start(s32[1024]{0:T(1024)} %param.11) | copy-start | bytes 12292
  7.2 56.5 %all-gather.9.cloned.1.call-start = ((), (), s32[]{:S(2)}) async-start(), calls=%async_computation.1 | async-start | bytes 2359296 | tf_op jit(solution)/shard_map/all_gather | solution.py:27
  9.0 74.1 %all-gather.11.cloned.1.call-start = ((), (), s32[]{:S(2)}) async-start(), calls=%async_computation.2 | async-start | bytes 1966080 | tf_op jit(solution)/shard_map/all_gather | solution.py:16
  9.8 251.7 %all-gather.13.cloned.1.call-start = ((), (), s32[]{:S(2)}) async-start(), calls=%async_computation.3 | async-start | bytes 14155776 | tf_op jit(solution)/shard_map/all_gather | solution.py:19
  10.5 302.2 %all-gather.15.cloned.1.call-start = ((), (), s32[]{:S(2)}) async-start(), calls=%async_computation.4 | async-start | bytes 2359296 | tf_op jit(solution)/shard_map/all_gather | solution.py:77
  12.4 375.2 %all-gather.7.cloned.1.call-start = ((), (), s32[]{:S(2)}) async-start(), calls=%async_computation | async-start | bytes 4718592 | tf_op jit(solution)/shard_map/all_gather | solution.py:44
  15.4 422.2 %all-gather.17.cloned.1.call-start = ((), (), s32[]{:S(2)}) async-start(), calls=%async_computation.5 | async-start | bytes 2359296 | tf_op jit(solution)/shard_map/all_gather | solution.py:78
  269.0 43.8 %copy-start.5 = (bf16[128,1024]{1,0:T(8,128)(2,1)S(1)}, bf16[128,1024]{1,0:T(8,128)(2,1)}, u32[]{:S(2)}) copy-start(bf16[128,1024]{1,0:T(8,128)(2,1)} %param.7) | copy-start | bytes 786436
  390.3 2.3 copy-start.4
  391.1 2.0 copy-start
  391.1 1.4 copy-start.1
  441.6 4.7 %copy-start.3 = (bf16[1024,1024]{0,1:T(8,128)(2,1)S(1)}, bf16[1024,1024]{0,1:T(8,128)(2,1)}, u32[]{:S(2)}) copy-start(bf16[1024,1024]{0,1:T(8,128)(2,1)} %all-gather.15.cloned.1.call-done) | copy-start | bytes 6291460
Sparse Core Ops, SparseCore 0:
  10.6 53.0 all-gather.8
  65.3 17.8 all-gather.10
  85.3 176.0 all-gather.12
  263.9 48.8 all-gather.14
  314.7 72.8 all-gather.6
  390.2 47.4 all-gather.16
